TPU v7x, 128 devices: a whole 4x4x4 slice. The times are simulated.
128 devices in a mesh: dp: 16 (over z, y_lo, core), expert: 8 (over x, y_hi).
Axes of the slice: x: 4, y: 4 (y_hi: 2, y_lo: 2; y = y_hi * 2 + y_lo), z: 4, core: 2. Of those that a mesh axis runs over, the one named last changes fastest.
Arguments:
- tokens: bfloat16 [16384, 4096], P(('dp', 'expert')), may hold values from -6 to 6
- expert_ids: int32 [16384, 2], P(('dp', 'expert')), may hold values from 0 to 7, all different within a row; in each aligned block of 128 rows (0 to 127, 128 to 255, ...) at most 80 rows name the same one
- gate_probs: float32 [16384, 2], P(('dp', 'expert')), may hold values from 0.2 to 1
- gate_weight: bfloat16 [8, 4096, 1536], P('expert', 'dp'), may hold values from -0.09375 to 0.09375
- up_weight: bfloat16 [8, 4096, 1536], P('expert', 'dp'), may hold values from -0.09375 to 0.09375
- down_weight: bfloat16 [8, 1536, 4096], P('expert', None, 'dp'), may hold values from -0.15625 to 0.15625
Outputs:
- mixed: bfloat16 [16384, 4096], P(('dp', 'expert'))
Inputs may be any that keep to these rules, and one draw needn't show every extreme that they name: `expert_ids`: each token names 2 different experts. Among the 128 tokens of one device (aligned blocks of rows), no expert is named by more than 80 tokens, and in every draw some expert is named by exactly 80 tokens of some device.
All inputs are finite; a program needn't handle non-finite values.
Results may differ from a plain program's by a relative error of at most 0.0057.
Values may be sent and summed in bfloat16 or wider, within the bound.
A program may use at most 128 MiB of HBM per device.

v0:
```python
import jax
import jax.numpy as jnp
from jax import lax
from jax.sharding import PartitionSpec as P

CAP = 80


def on_device(tokens, expert_ids, gate_probs, gate_weight, up_weight, down_weight):
    tok_count, model_width = tokens.shape
    top_count = expert_ids.shape[1]
    groups = lax.axis_size("expert")
    total_rows = groups * CAP
    flat_ids = expert_ids.reshape(-1)
    onehot = (flat_ids[:, None] == jnp.arange(groups, dtype=jnp.int32)[None, :]).astype(jnp.int32)
    ranks = jnp.cumsum(onehot, axis=0) - 1
    rank_own = jnp.sum(ranks * onehot, axis=1)
    slot_index = flat_ids * CAP + rank_own
    counts = jnp.sum(onehot, axis=0)
    source_rows = jnp.arange(tok_count * top_count, dtype=jnp.int32) // top_count
    table = jnp.full((total_rows,), tok_count, jnp.int32).at[slot_index].set(source_rows)
    padded_tokens = jnp.concatenate([tokens, jnp.zeros((1, model_width), tokens.dtype)], axis=0)
    send_rows = padded_tokens[table]
    received, arrived = (
        lax.all_to_all(send_rows, "expert", split_axis=0, concat_axis=0, tiled=True),
        lax.all_to_all(counts[:, None], "expert", split_axis=0, concat_axis=0, tiled=True),
    )
    arrived = arrived[:, 0]
    gate_local = gate_weight[0]
    up_local = up_weight[0]
    down_local = down_weight[0]
    gate = jnp.dot(
        received,
        lax.all_gather(gate_local, "dp", axis=0, tiled=True),
        preferred_element_type=jnp.float32,
    )
    upper = jnp.dot(
        received,
        lax.all_gather(up_local, "dp", axis=0, tiled=True),
        preferred_element_type=jnp.float32,
    )
    hidden = (jax.nn.silu(gate) * upper).astype(jnp.bfloat16)
    outputs = jnp.dot(
        hidden,
        lax.all_gather(down_local, "dp", axis=1, tiled=True),
        preferred_element_type=jnp.float32,
    ).astype(jnp.bfloat16)
    returned = lax.all_to_all(outputs, "expert", split_axis=0, concat_axis=0, tiled=True)
    picked = returned[slot_index].astype(jnp.float32)
    weighted = picked * gate_probs.reshape(-1)[:, None]
    mixed = jnp.sum(weighted.reshape(tok_count, top_count, model_width), axis=1)
    return mixed.astype(jnp.bfloat16)


def solution(mesh):
    placed = (
        P(("dp", "expert"), None),
        P(("dp", "expert"), None),
        P(("dp", "expert"), None),
        P("expert", "dp", None),
        P("expert", "dp", None),
        P("expert", None, "dp"),
    )
    return jax.shard_map(
        on_device, mesh=mesh, in_specs=placed, out_specs=P(("dp", "expert"), None), check_vma=False
    )
```

profile of v0, /device:TPU:1, one launch (start us, length us, event | category | flops | bytes accessed | tf_op | source)
XLA Modules:
  0.0 431.1 jit_solution(3689289020772454636)
XLA Ops:
  6.5 0.0 all-gather.7.cloned.1.call-start
  6.5 0.7 all-gather.7.cloned.1.call-update
  7.3 0.0 all-gather.11.cloned.1.call-start
  7.3 0.7 all-gather.11.cloned.1.call-update
  8.0 0.0 all-gather.9.cloned.1.call-start
  8.1 0.7 all-gather.9.cloned.1.call-update
  8.7 0.8 copy.9
  9.5 0.1 eq.29
  9.7 0.1 eq.25
  9.8 0.6 reduce-window.6
  10.4 0.2 slice_reduce_fusion
  10.7 0.7 broadcast_multiply_fusion
  11.4 0.1 copy.8
  11.5 0.1 mul.37
  11.6 1.3 concatenate.3
  13.0 0.1 fusion.14
  13.1 0.0 copy-start
  13.1 1.4 scatter_custom_fusion
  14.5 5.4 %gather_fusion = bf16[640,4096]{1,0:T(8,128)(2,1)} fusion(bf16[129,4096]{1,0:T(8,128)(2,1)S(1)} %concatenate.3, s32[1024]{0:T(1024)S(1)} %pad_clamp_fusion.1), kind=kCustom, calls=%fused_computation | custom fusion | bytes 10488320 | tf_op jit(solution)/shard_map/gather | solution.py:23
  19.9 0.0 copy-done
  19.9 81.7 %all_to_all.24 = bf16[8,80,4096]{2,1,0:T(8,128)(2,1)} all-to-all(bf16[8,80,4096]{2,1,0:T(8,128)(2,1)} %bitcast.29), channel_id=1, replica_groups=mesh['dp'=16,'expert'=8] {'expert'}, dimensions={0} | all-to-all | bytes 10485760 | tf_op jit(solution)/shard_map/all_to_all | solution.py:25
  101.6 39.0 %all-gather.7.cloned.1.call-done = bf16[1,4096,1536]{2,1,0:T(8,128)(2,1)} async-done(((bf16[1,256,1536]{2,1,0:T(8,128)(2,1)}), bf16[1,4096,1536]{2,1,0:T(8,128)(2,1)}) %all-gather.7.cloned.1.call-update) | async-done | bytes 12582928 | tf_op jit(solution)/shard_map/all_gather | solution.py:34
  140.6 14.1 %fusion.4 = f32[640,1536]{1,0:T(8,128)} fusion(bf16[640,4096]{1,0:T(8,128)(2,1)} %bitcast.30, bf16[1,4096,1536]{2,1,0:T(8,128)(2,1)} %all-gather.7.cloned.1.call-done), kind=kOutput, calls=%fused_computation.7 | convolution fusion | flops 8053063680 | bytes 21757952 | tf_op jit(solution)/shard_map/dot_general | solution.py:32
  154.7 67.9 %all-gather.11.cloned.1.call-done = bf16[1,1536,4096]{2,1,0:T(8,128)(2,1)} async-done(((bf16[1,1536,256]{2,1,0:T(8,128)(2,1)}), bf16[1,1536,4096]{2,1,0:T(8,128)(2,1)}) %all-gather.11.cloned.1.call-update) | async-done | bytes 12582928 | tf_op jit(solution)/shard_map/all_gather | solution.py:45
  222.6 73.6 %all-gather.9.cloned.1.call-done = bf16[1,4096,1536]{2,1,0:T(8,128)(2,1)} async-done(((bf16[1,256,1536]{2,1,0:T(8,128)(2,1)}), bf16[1,4096,1536]{2,1,0:T(8,128)(2,1)}) %all-gather.9.cloned.1.call-update) | async-done | bytes 12582928 | tf_op jit(solution)/shard_map/all_gather | solution.py:39
  296.2 27.9 %fusion.6 = bf16[640,4096]{1,0:T(8,128)(2,1)} fusion(bf16[1,1536,4096]{2,1,0:T(8,128)(2,1)} %all-gather.11.cloned.1.call-done, f32[640,1536]{1,0:T(8,128)} %fusion.4, bf16[640,4096]{1,0:T(8,128)(2,1)} %bitcast.31, bf16[1,4096,1536]{2,1,0:T(8,128)(2,1)} %all-gather.9.cloned.1.call-done), kind=kOutput, calls=%fused_computation.9 | convolution fusion | flops 16114647040 | bytes 39583744 | tf_op jit(solution)/shard_map/dot_general | solution.py:43
  324.1 0.0 copy-start.2
  324.1 0.0 copy-start.1
  324.1 6.6 %all-to-all-start.1 = ((bf16[8,80,4096]{2,1,0:T(8,128)(2,1)}), bf16[8,80,4096]{2,1,0:T(8,128)(2,1)}, u32[]{:S(2)}, u32[]{:S(2)}) async-start(bf16[8,80,4096]{2,1,0:T(8,128)(2,1)} %bitcast.32), calls=%async_computation.1 | async-start | bytes 10485760 | tf_op jit(solution)/shard_map/all_to_all | solution.py:48
  330.7 0.0 copy-done.2
  330.7 0.1 copy.11
  330.8 0.0 copy-done.1
  330.8 73.1 %all-to-all-done.1 = bf16[8,80,4096]{2,1,0:T(8,128)(2,1)} async-done(((bf16[8,80,4096]{2,1,0:T(8,128)(2,1)}), bf16[8,80,4096]{2,1,0:T(8,128)(2,1)}, u32[]{:S(2)}, u32[]{:S(2)}) %all-to-all-start.1) | async-done | bytes 5242912 | tf_op jit(solution)/shard_map/all_to_all | solution.py:48
  403.9 7.0 %gather_fusion.1 = bf16[256,4096]{1,0:T(8,128)(2,1)S(1)} fusion(bf16[640,4096]{1,0:T(8,128)(2,1)} %bitcast.10, s32[1024]{0:T(1024)S(1)} %pad_clamp_fusion), kind=kCustom, calls=%fused_computation.1 | custom fusion | bytes 4195328 | tf_op jit(solution)/shard_map/gather | solution.py:49
  410.9 4.0 reshape.63
  414.9 9.6 %multiply_reduce_fusion = bf16[128,4096]{1,0:T(8,128)(2,1)} fusion(f32[128,2,4096]{2,1,0:T(2,128)} %reshape.63, f32[128,2]{1,0:T(8,128)S(1)} %copy.11), kind=kLoop, calls=%fused_computation.10 | loop fusion | flops 1572864 | bytes 5243904 | tf_op jit(solution)/shard_map/reduce_sum | solution.py:51
  (8 shorter events, 0.1 us)
Async XLA Ops:
  6.5 134.1 %all-gather.7.cloned.1.call-start = ((), (), s32[]{:S(2)}) async-start(), calls=%async_computation.2 | async-start | bytes 13369344 | tf_op jit(solution)/shard_map/all_gather | solution.py:34
  7.3 215.4 %all-gather.11.cloned.1.call-start = ((), (), s32[]{:S(2)}) async-start(), calls=%async_computation.4 | async-start | bytes 13369344 | tf_op jit(solution)/shard_map/all_gather | solution.py:45
  8.0 288.2 %all-gather.9.cloned.1.call-start = ((), (), s32[]{:S(2)}) async-start(), calls=%async_computation.3 | async-start | bytes 13369344 | tf_op jit(solution)/shard_map/all_gather | solution.py:39
  13.1 6.9 %copy-start = (s32[256,1]{0,1:T(1,128)}, s32[256,1]{0,1:T(1,128)S(1)}, u32[]{:S(2)}) copy-start(s32[256,1]{0,1:T(1,128)S(1)} %compare_select_fusion.1) | copy-start | bytes 3076
  324.1 6.6 %copy-start.2 = (f32[128,2]{0,1:T(2,128)S(1)}, f32[128,2]{0,1:T(2,128)}, u32[]{:S(2)}) copy-start(f32[128,2]{0,1:T(2,128)} %param.8) | copy-start | bytes 3076
  324.1 6.7 %copy-start.1 = (s32[256,1]{0,1:T(1,128)S(1)}, s32[256,1]{0,1:T(1,128)}, u32[]{:S(2)}) copy-start(s32[256,1]{0,1:T(1,128)} %copy-done) | copy-start | bytes 3076
  324.1 79.8 %all-to-all-start.1 = ((bf16[8,80,4096]{2,1,0:T(8,128)(2,1)}), bf16[8,80,4096]{2,1,0:T(8,128)(2,1)}, u32[]{:S(2)}, u32[]{:S(2)}) async-start(bf16[8,80,4096]{2,1,0:T(8,128)(2,1)} %bitcast.32), calls=%async_computation.1 | async-start | bytes 10485760 | tf_op jit(solution)/shard_map/all_to_all | solution.py:48
Sparse Core Ops, SparseCore 0:
  9.1 131.5 all-gather.6
  142.2 80.3 all-gather.10
  224.3 71.8 all-gather.8
where the time goes:
time: 432 us; the launch traced here: 431 us
  waiting for transfers between devices  256 us (59%)
  blocking collectives  81.7 us (19%)
  matrix products  41.9 us (10%)
  local copies, waits for them, and re-layouts  20.8 us (5%)
  between operations  13.2 us (3%)
  other arithmetic  11.1 us (3%)
  starting transfers between devices  6.64 us (2%)
    all_to_all x1, blocking collectives, on_device(): lax.all_to_all(send_rows, 'expert', split_axis=0, concat_axis=0, tiled=True)  81.7 us
    all_gather x1, waiting for transfers between devices, on_device(): lax.all_gather(up_local, 'dp', axis=0, tiled=True)  73.6 us
    all_to_all x1, waiting for transfers between devices, on_device(): lax.all_to_all(outputs, 'expert', split_axis=0, concat_axis=0, tiled=True)  73.1 us
    all_gather x1, waiting for transfers between devices, on_device(): lax.all_gather(down_local, 'dp', axis=1, tiled=True)  67.9 us
    all_gather x1, waiting for transfers between devices, on_device(): lax.all_gather(gate_local, 'dp', axis=0, tiled=True)  39 us
    dot_general x1, matrix products, on_device(): jnp.dot(hidden, lax.all_gather(down_local, 'dp', axis=1, tiled=True), pre...  27.9 us
    dot_general x1, matrix products, on_device(): jnp.dot(received, lax.all_gather(gate_local, 'dp', axis=0, tiled=True), p...  14.1 us
    reduce_sum x1, other arithmetic, on_device(): mixed = jnp.sum(weighted.reshape(tok_count, top_count, model_width), axis=1)  9.64 us
  transfers between devices with their start and end apart: 4, of which 4 were waited for; matrix products, arithmetic and copies ran while one was open for 6% of the time, Pallas kernels for 0%

commit v1 on v0

--- a/solution.py
+++ b/solution.py
@@ -42,7 +42,15 @@
     hidden = (jax.nn.silu(gate) * upper).astype(jnp.bfloat16)
     outputs = jnp.dot(
         hidden,
-        lax.all_gather(down_local, "dp", axis=1, tiled=True),
+        jnp.concatenate(
+            lax.all_to_all(
+                jnp.stack([down_local] * lax.axis_size("dp")),
+                axis_name="dp",
+                split_axis=0,
+                concat_axis=0,
+            ),
+            axis=1,
+        ),
         preferred_element_type=jnp.float32,
     ).astype(jnp.bfloat16)
     returned = lax.all_to_all(outputs, "expert", split_axis=0, concat_axis=0, tiled=True)

time: 432 us -> 492 us (1.14)
  waiting for transfers between devices: 256 us -> 370 us
  blocking collectives: 81.7 us -> 0 us
  starting transfers between devices: 6.64 us -> 24.3 us
  local copies, waits for them, and re-layouts: 20.8 us -> 26.9 us
    all_to_all x0 -> x2, waiting for transfers between devices: none -> 223 us  [the longest x1 149 us: on_device(): lax.all_to_all(jnp.stack([down_local] * lax.axis_size('dp')), axis_name='...]
    all_to_all x1 -> x0, blocking collectives: 81.7 us -> none  [on_device(): lax.all_to_all(send_rows, 'expert', split_axis=0, concat_axis=0, tiled=True)]
    all_gather x1 -> x0, waiting for transfers between devices: 67.9 us -> none  [on_device(): lax.all_gather(down_local, 'dp', axis=1, tiled=True)]
    all_gather x1, waiting for transfers between devices: 73.6 us -> 6.45 us  [on_device(): lax.all_gather(up_local, 'dp', axis=0, tiled=True)]
    all_gather x1, waiting for transfers between devices: 39 us -> 66.8 us  [on_device(): lax.all_gather(gate_local, 'dp', axis=0, tiled=True)]
    all_to_all x0 -> x2, starting transfers between devices: none -> 14.9 us  [the longest x1 7.61 us: on_device(): lax.all_to_all(send_rows, 'expert', split_axis=0, concat_axis=0, tiled=True)]
    another operation x1 -> x3, local copies, waits for them, and re-layouts: 0.01 us -> 5.94 us  [the longest x1 5.66 us: on_device(): jnp.stack([down_local] * lax.axis_size('dp'))]
  transfers between devices with their start and end apart: 4 -> 5, of which waited for: 4 -> 5; matrix products, arithmetic and copies ran while one was open for 6% -> 6% of each run, Pallas kernels for 0% -> 0%
where the time goes in v1:
time: 492 us; the launch traced here: 486 us
  waiting for transfers between devices  370 us (75%)
  matrix products  40.2 us (8%)
  local copies, waits for them, and re-layouts  26.9 us (5%)
  starting transfers between devices  24.3 us (5%)
  between operations  13.5 us (3%)
  other arithmetic  11.1 us (2%)
    all_to_all x1, waiting for transfers between devices, on_device(): lax.all_to_all(jnp.stack([down_local] * lax.axis_size('dp')), axis_name='...  149 us
    all_to_all x1, waiting for transfers between devices, on_device(): lax.all_to_all(send_rows, 'expert', split_axis=0, concat_axis=0, tiled=True)  74 us
    all_to_all x1, waiting for transfers between devices, on_device(): lax.all_to_all(outputs, 'expert', split_axis=0, concat_axis=0, tiled=True)  72.7 us
    all_gather x1, waiting for transfers between devices, on_device(): lax.all_gather(gate_local, 'dp', axis=0, tiled=True)  66.8 us
    dot_general x1, matrix products, on_device(): jnp.dot(hidden, jnp.concatenate(lax.all_to_all(jnp.stack([down_local] * l...  26.1 us
    dot_general x1, matrix products, on_device(): jnp.dot(received, lax.all_gather(gate_local, 'dp', axis=0, tiled=True), p...  14.1 us
  transfers between devices with their start and end apart: 5, of which 5 were waited for; matrix products, arithmetic and copies ran while one was open for 6% of the time, Pallas kernels for 0%

profile of v1, /device:TPU:1, one launch (start us, length us, event | category | flops | bytes accessed | tf_op | source)
XLA Modules:
  0.0 486.2 jit_solution(11354025230426715989)
XLA Ops:
  6.5 0.0 all-gather.5.cloned.1.call-start
  6.5 0.7 all-gather.5.cloned.1.call-update
  7.3 0.0 all-gather.7.cloned.1.call-start
  7.3 0.7 all-gather.7.cloned.1.call-update
  8.0 0.8 copy.9
  8.8 0.1 eq.29
  8.9 0.1 eq.25
  9.1 0.6 reduce-window.6
  9.7 0.2 slice_reduce_fusion
  9.9 0.7 broadcast_multiply_fusion
  10.6 0.1 copy.8
  10.7 0.1 mul.37
  10.9 1.3 concatenate.3
  12.2 0.1 fusion.9
  12.3 0.0 copy-start.1
  12.3 1.4 scatter_custom_fusion
  13.8 5.5 %gather_fusion = bf16[640,4096]{1,0:T(8,128)(2,1)} fusion(bf16[129,4096]{1,0:T(8,128)(2,1)S(1)} %concatenate.3, s32[1024]{0:T(1024)S(1)} %pad_clamp_fusion.1), kind=kCustom, calls=%fused_computation | custom fusion | bytes 10488320 | tf_op jit(solution)/shard_map/gather | solution.py:23
  19.3 0.0 copy-done.1
  19.3 0.0 copy-start
  19.3 7.6 %all-to-all-start = ((bf16[8,80,4096]{2,1,0:T(8,128)(2,1)}), bf16[8,80,4096]{2,1,0:T(8,128)(2,1)}, u32[]{:S(2)}, u32[]{:S(2)}) async-start(bf16[8,80,4096]{2,1,0:T(8,128)(2,1)} %bitcast.29), calls=%async_computation | async-start | bytes 10485760 | tf_op jit(solution)/shard_map/all_to_all | solution.py:25
  26.9 0.0 copy-done
  26.9 0.3 copy.11
  27.2 74.0 %all-to-all-done = bf16[8,80,4096]{2,1,0:T(8,128)(2,1)} async-done(((bf16[8,80,4096]{2,1,0:T(8,128)(2,1)}), bf16[8,80,4096]{2,1,0:T(8,128)(2,1)}, u32[]{:S(2)}, u32[]{:S(2)}) %all-to-all-start) | async-done | bytes 5242912 | tf_op jit(solution)/shard_map/all_to_all | solution.py:25
  101.1 5.7 %stack.3 = bf16[16,1536,256]{1,2,0:T(8,128)(2,1)} broadcast(bf16[1536,256]{0,1:T(8,128)(2,1)S(1)} %copy.11), dimensions={1,2} | broadcast | bytes 13369344 | tf_op jit(solution)/shard_map/stack | solution.py:47
  106.8 7.2 %all-to-all-start.1 = ((bf16[16,1536,256]{1,2,0:T(8,128)(2,1)}), bf16[16,1536,256]{1,2,0:T(8,128)(2,1)}, u32[]{:S(2)}, u32[]{:S(2)}) async-start(bf16[16,1536,256]{1,2,0:T(8,128)(2,1)} %stack.3), calls=%async_computation.1 | async-start | bytes 25165824 | tf_op jit(solution)/shard_map/all_to_all | solution.py:46
  114.0 66.8 %all-gather.5.cloned.1.call-done = bf16[1,4096,1536]{2,1,0:T(8,128)(2,1)} async-done(((bf16[1,256,1536]{2,1,0:T(8,128)(2,1)}), bf16[1,4096,1536]{2,1,0:T(8,128)(2,1)}) %all-gather.5.cloned.1.call-update) | async-done | bytes 12582928 | tf_op jit(solution)/shard_map/all_gather | solution.py:34
  180.8 14.1 %fusion.2 = f32[640,1536]{1,0:T(8,128)} fusion(bf16[640,4096]{1,0:T(8,128)(2,1)} %bitcast.5, bf16[1,4096,1536]{2,1,0:T(8,128)(2,1)} %all-gather.5.cloned.1.call-done), kind=kOutput, calls=%fused_computation.5 | convolution fusion | flops 8053063680 | bytes 21757952 | tf_op jit(solution)/shard_map/dot_general | solution.py:32
  195.0 148.9 %all-to-all-done.1 = bf16[16,1536,256]{1,2,0:T(8,128)(2,1)} async-done(((bf16[16,1536,256]{1,2,0:T(8,128)(2,1)}), bf16[16,1536,256]{1,2,0:T(8,128)(2,1)}, u32[]{:S(2)}, u32[]{:S(2)}) %all-to-all-start.1) | async-done | bytes 12582944 | tf_op jit(solution)/shard_map/all_to_all | solution.py:46
  343.9 6.5 %all-gather.7.cloned.1.call-done = bf16[1,4096,1536]{2,1,0:T(8,128)(2,1)} async-done(((bf16[1,256,1536]{2,1,0:T(8,128)(2,1)}), bf16[1,4096,1536]{2,1,0:T(8,128)(2,1)}) %all-gather.7.cloned.1.call-update) | async-done | bytes 12582928 | tf_op jit(solution)/shard_map/all_gather | solution.py:39
  350.4 26.1 %convolution_convert_fusion = bf16[640,4096]{1,0:T(8,128)(2,1)} fusion(bf16[1536,4096]{0,1:T(8,128)(2,1)} %bitcast.10, f32[640,1536]{1,0:T(8,128)} %fusion.2, bf16[640,4096]{1,0:T(8,128)(2,1)} %bitcast.5, bf16[1,4096,1536]{2,1,0:T(8,128)(2,1)} %all-gather.7.cloned.1.call-done), kind=kOutput, calls=%fused_computation.7 | convolution fusion | flops 16114647040 | bytes 39583744 | tf_op jit(solution)/shard_map/dot_general | solution.py:43
  376.4 0.0 copy-start.3
  376.4 0.0 copy-start.2
  376.4 9.4 %all-to-all-start.2 = ((bf16[8,80,4096]{2,1,0:T(8,128)(2,1)}), bf16[8,80,4096]{2,1,0:T(8,128)(2,1)}, u32[]{:S(2)}, u32[]{:S(2)}) async-start(bf16[8,80,4096]{2,1,0:T(8,128)(2,1)} %bitcast.30), calls=%async_computation.2 | async-start | bytes 10485760 | tf_op jit(solution)/shard_map/all_to_all | solution.py:56
  385.8 0.0 copy-done.3
  385.9 0.1 copy.12
  386.0 0.0 copy-done.2
  386.0 72.7 %all-to-all-done.2 = bf16[8,80,4096]{2,1,0:T(8,128)(2,1)} async-done(((bf16[8,80,4096]{2,1,0:T(8,128)(2,1)}), bf16[8,80,4096]{2,1,0:T(8,128)(2,1)}, u32[]{:S(2)}, u32[]{:S(2)}) %all-to-all-start.2) | async-done | bytes 5242912 | tf_op jit(solution)/shard_map/all_to_all | solution.py:56
  458.7 7.0 %gather_fusion.1 = bf16[256,4096]{1,0:T(8,128)(2,1)S(1)} fusion(bf16[640,4096]{1,0:T(8,128)(2,1)} %bitcast.12, s32[1024]{0:T(1024)S(1)} %pad_clamp_fusion), kind=kCustom, calls=%fused_computation.1 | custom fusion | bytes 4195328 | tf_op jit(solution)/shard_map/gather | solution.py:57
  465.8 4.0 reshape.72
  469.8 9.6 %multiply_reduce_fusion = bf16[128,4096]{1,0:T(8,128)(2,1)} fusion(f32[128,2,4096]{2,1,0:T(2,128)} %reshape.72, f32[128,2]{1,0:T(8,128)S(1)} %copy.12), kind=kLoop, calls=%fused_computation.8 | loop fusion | flops 1572864 | bytes 5243904 | tf_op jit(solution)/shard_map/reduce_sum | solution.py:59
  (8 shorter events, 0.1 us)
Async XLA Ops:
  6.5 174.3 %all-gather.5.cloned.1.call-start = ((), (), s32[]{:S(2)}) async-start(), calls=%async_computation.3 | async-start | bytes 13369344 | tf_op jit(solution)/shard_map/all_gather | solution.py:34
  7.3 343.1 %all-gather.7.cloned.1.call-start = ((), (), s32[]{:S(2)}) async-start(), calls=%async_computation.4 | async-start | bytes 13369344 | tf_op jit(solution)/shard_map/all_gather | solution.py:39
  12.3 6.9 %copy-start.1 = (s32[256,1]{0,1:T(1,128)}, s32[256,1]{0,1:T(1,128)S(1)}, u32[]{:S(2)}) copy-start(s32[256,1]{0,1:T(1,128)S(1)} %compare_select_fusion.1) | copy-start | bytes 3076
  19.3 7.6 %copy-start = (bf16[1,1536,256]{2,1,0:T(8,128)(2,1)S(1)}, bf16[1,1536,256]{2,1,0:T(8,128)(2,1)}, u32[]{:S(2)}) copy-start(bf16[1,1536,256]{2,1,0:T(8,128)(2,1)} %param.11) | copy-start | bytes 2359300
  19.3 81.8 %all-to-all-start = ((bf16[8,80,4096]{2,1,0:T(8,128)(2,1)}), bf16[8,80,4096]{2,1,0:T(8,128)(2,1)}, u32[]{:S(2)}, u32[]{:S(2)}) async-start(bf16[8,80,4096]{2,1,0:T(8,128)(2,1)} %bitcast.29), calls=%async_computation | async-start | bytes 10485760 | tf_op jit(solution)/shard_map/all_to_all | solution.py:25
  106.8 237.1 %all-to-all-start.1 = ((bf16[16,1536,256]{1,2,0:T(8,128)(2,1)}), bf16[16,1536,256]{1,2,0:T(8,128)(2,1)}, u32[]{:S(2)}, u32[]{:S(2)}) async-start(bf16[16,1536,256]{1,2,0:T(8,128)(2,1)} %stack.3), calls=%async_computation.1 | async-start | bytes 25165824 | tf_op jit(solution)/shard_map/all_to_all | solution.py:46
  376.4 9.4 %copy-start.3 = (f32[128,2]{0,1:T(2,128)S(1)}, f32[128,2]{0,1:T(2,128)}, u32[]{:S(2)}) copy-start(f32[128,2]{0,1:T(2,128)} %param.8) | copy-start | bytes 3076
  376.4 9.6 %copy-start.2 = (s32[256,1]{0,1:T(1,128)S(1)}, s32[256,1]{0,1:T(1,128)}, u32[]{:S(2)}) copy-start(s32[256,1]{0,1:T(1,128)} %copy-done.1) | copy-start | bytes 3076
  376.4 82.3 %all-to-all-start.2 = ((bf16[8,80,4096]{2,1,0:T(8,128)(2,1)}), bf16[8,80,4096]{2,1,0:T(8,128)(2,1)}, u32[]{:S(2)}, u32[]{:S(2)}) async-start(bf16[8,80,4096]{2,1,0:T(8,128)(2,1)} %bitcast.30), calls=%async_computation.2 | async-start | bytes 10485760 | tf_op jit(solution)/shard_map/all_to_all | solution.py:56
Sparse Core Ops, SparseCore 0:
  9.1 171.7 all-gather.4
  182.5 167.7 all-gather.6
